TPU v7x, 32 devices: a whole 2x2x4 slice. The times are simulated.
32 devices in a mesh: pos: 8 (over z, y), fr: 4 (over x, core).
Axes of the slice: x: 2, y: 2, z: 4, core: 2. Of those that a mesh axis runs over, the one named last changes fastest.
Arguments:
- inputs: bfloat16 [8, 2048, 1024], P('pos', 'fr'), may hold values from -6 to 6
- delays: int32 [32, 8], P('fr', 'pos'), may hold values from 0 to 2
- query_weight: bfloat16 [8, 1024, 1024], P('pos', 'fr'), may hold values from -0.1875 to 0.1875
- key_weight: bfloat16 [8, 1024, 1024], P('pos', 'fr'), may hold values from -0.1875 to 0.1875
- value_weight: bfloat16 [8, 1024, 1024], P('pos', 'fr'), may hold values from -0.1875 to 0.1875
- out_weight: bfloat16 [8, 1024, 1024], P('pos', 'fr'), may hold values from -0.375 to 0.375
- gate_weight: bfloat16 [8, 1024, 2816], P('pos', 'fr'), may hold values from -0.1875 to 0.1875
- up_weight: bfloat16 [8, 1024, 2816], P('pos', 'fr'), may hold values from -0.1875 to 0.1875
- down_weight: bfloat16 [8, 2816, 1024], P('pos', 'fr'), may hold values from -0.109375 to 0.109375
- attention_gain: bfloat16 [8, 1024], P('pos', 'fr'), may hold values from 0.099609375 to 1.8984375
- feed_gain: bfloat16 [8, 1024], P('pos', 'fr'), may hold values from 0.099609375 to 1.8984375
- cotangent: bfloat16 [8, 2048, 1024], P('pos', 'fr'), may hold values from -6 to 6
Outputs:
- output: bfloat16 [8, 2048, 1024], P('pos', 'fr')
- input_grad: bfloat16 [8, 2048, 1024], P('pos', 'fr')
- query_weight_grad: float32 [8, 1024, 1024], P('pos', 'fr')
- key_weight_grad: float32 [8, 1024, 1024], P('pos', 'fr')
- value_weight_grad: float32 [8, 1024, 1024], P('pos', 'fr')
- out_weight_grad: float32 [8, 1024, 1024], P('pos', 'fr')
- gate_weight_grad: float32 [8, 1024, 2816], P('pos', 'fr')
- up_weight_grad: float32 [8, 1024, 2816], P('pos', 'fr')
- down_weight_grad: float32 [8, 2816, 1024], P('pos', 'fr')
- attention_gain_grad: float32 [8, 1024], P('pos', 'fr')
- feed_gain_grad: float32 [8, 1024], P('pos', 'fr')
All inputs are finite; a program needn't handle non-finite values.
Results may differ from a plain program's by a relative error of at most 0.02.
Values may be sent and summed in bfloat16 or wider, within the bound.
A program may use at most 256 MiB of HBM per device.

v0:
```python
import jax
import jax.numpy as jnp
from jax import lax
from jax.sharding import PartitionSpec as P

HEAD = 64
EPSILON = 1e-06
NEGATIVE = -1e30


def shifted(x, axis, by):
    peers = lax.axis_size(axis)
    pairs = [(i, i + by) for i in range(peers) if 0 <= i + by < peers]
    return lax.ppermute(x, axis, pairs)


def rms_scaling(values):
    return lax.rsqrt(jnp.mean(values * values, -1, keepdims=True) + EPSILON)


def product(operand, weight):
    return jnp.dot(operand, weight, preferred_element_type=jnp.float32)


def outer_sum(operand, second):
    return lax.dot_general(
        operand, second, (((0,), (0,)), ((), ())), preferred_element_type=jnp.float32
    )


def back_product(grad_rows, weight):
    return lax.dot_general(
        grad_rows, weight, (((1,), (1,)), ((), ())), preferred_element_type=jnp.float32
    )


def norm_back(values, scaling, gain_row, grad_normed):
    weighted = gain_row * grad_normed
    return scaling * weighted - values * scaling**3 * jnp.mean(weighted * values, -1, keepdims=True)


def project_in(hidden, weights):
    scaling = rms_scaling(hidden)
    normed = (hidden * scaling * weights[7].astype(jnp.float32)).astype(jnp.bfloat16)
    queries = product(normed, weights[0]).astype(jnp.bfloat16)
    key_rows = product(normed, weights[1]).astype(jnp.bfloat16)
    value_rows = product(normed, weights[2]).astype(jnp.bfloat16)
    return (scaling, normed, queries, key_rows, value_rows)


def attend(queries, keys_all, values_all, position, logsum):
    frames = queries.shape[0]
    head_count = queries.shape[1] // HEAD
    positions = keys_all.shape[0]
    query_heads = queries.reshape(frames, head_count, HEAD)
    key_heads = keys_all.reshape(positions, frames, head_count, HEAD)
    value_heads = values_all.reshape(positions, frames, head_count, HEAD)
    scores = jnp.einsum(
        "fhe,jfhe->fhj", query_heads, key_heads, preferred_element_type=jnp.float32
    ) * HEAD ** (-0.5)
    allowed = jnp.arange(positions) <= position
    scores = jnp.where(allowed, scores, NEGATIVE)
    if logsum is None:
        highest = jnp.max(scores, -1, keepdims=True)
        logsum = highest + jnp.log(jnp.sum(jnp.exp(scores - highest), -1, keepdims=True))
    soft_weights = jnp.exp(scores - logsum)
    soft_low = soft_weights.astype(jnp.bfloat16)
    attended = jnp.einsum(
        "fhj,jfhe->fhe", soft_low, value_heads, preferred_element_type=jnp.float32
    )
    attended = attended.astype(jnp.bfloat16).reshape(frames, -1)
    return (attended, logsum, soft_weights, soft_low)


def finish(hidden, attended, weights):
    branch = hidden + product(attended, weights[3])
    scaling_two = rms_scaling(branch)
    normed_two = (branch * scaling_two * weights[8].astype(jnp.float32)).astype(jnp.bfloat16)
    gate_act = product(normed_two, weights[4])
    up_act = product(normed_two, weights[5])
    inner_act = (jax.nn.silu(gate_act) * up_act).astype(jnp.bfloat16)
    return (branch, scaling_two, normed_two, gate_act, up_act, inner_act)


def on_device(
    inputs,
    delays,
    query_weight,
    key_weight,
    value_weight,
    out_weight,
    gate_weight,
    up_weight,
    down_weight,
    attention_gain,
    feed_gain,
    cotangent,
):
    position = lax.axis_index("pos")
    own_rows = inputs[0]
    frames = own_rows.shape[0]
    rim_rows = shifted(own_rows[frames - 2 :], "fr", 1)
    extended = jnp.concatenate([rim_rows, own_rows], 0)
    lag_rows = jnp.repeat(delays[:, 0], frames // delays.shape[0])[:, None]
    hidden = jnp.where(
        lag_rows == 0,
        extended[2:],
        jnp.where(lag_rows == 1, extended[1 : frames + 1], extended[:frames]),
    )
    hidden = hidden.astype(jnp.float32)
    gathered = (
        lax.all_gather(query_weight, "fr", axis=1, tiled=True),
        lax.all_gather(key_weight, "fr", axis=1, tiled=True),
        lax.all_gather(value_weight, "fr", axis=1, tiled=True),
        lax.all_gather(out_weight, "fr", axis=1, tiled=True),
        lax.all_gather(gate_weight, "fr", axis=1, tiled=True),
        lax.all_gather(up_weight, "fr", axis=1, tiled=True),
        lax.all_gather(down_weight, "fr", axis=1, tiled=True),
        lax.all_gather(attention_gain, "fr", axis=1, tiled=True),
        lax.all_gather(feed_gain, "fr", axis=1, tiled=True),
    )
    forward_weights = tuple((shard_piece[0] for shard_piece in gathered))
    scaling, normed, queries, key_rows, value_rows = project_in(hidden, forward_weights)
    keys_all, values_all = (
        lax.all_gather(key_rows[None], "pos", axis=0, tiled=True),
        lax.all_gather(value_rows[None], "pos", axis=0, tiled=True),
    )
    attended, logsum, soft_weights, soft_low = attend(queries, keys_all, values_all, position, None)
    branch, scaling_two, normed_two, gate_act, up_act, inner_act = finish(
        hidden, attended, forward_weights
    )
    output = (branch + product(inner_act, forward_weights[6])).astype(jnp.bfloat16)
    regathered = (
        lax.all_gather(query_weight, "fr", axis=1, tiled=True),
        lax.all_gather(key_weight, "fr", axis=1, tiled=True),
        lax.all_gather(value_weight, "fr", axis=1, tiled=True),
        lax.all_gather(out_weight, "fr", axis=1, tiled=True),
        lax.all_gather(gate_weight, "fr", axis=1, tiled=True),
        lax.all_gather(up_weight, "fr", axis=1, tiled=True),
        lax.all_gather(down_weight, "fr", axis=1, tiled=True),
        lax.all_gather(attention_gain, "fr", axis=1, tiled=True),
        lax.all_gather(feed_gain, "fr", axis=1, tiled=True),
    )
    backward_weights = tuple((shard_piece[0] for shard_piece in regathered))
    scaling, normed, queries, key_rows, value_rows = project_in(hidden, backward_weights)
    keys_all, values_all = (
        lax.all_gather(key_rows[None], "pos", axis=0, tiled=True),
        lax.all_gather(value_rows[None], "pos", axis=0, tiled=True),
    )
    attended, logsum, soft_weights, soft_low = attend(
        queries, keys_all, values_all, position, logsum
    )
    branch, scaling_two, normed_two, gate_act, up_act, inner_act = finish(
        hidden, attended, backward_weights
    )
    (
        query_full,
        key_full,
        value_full,
        out_full,
        gate_full,
        up_full,
        down_full,
        gain_one,
        gain_two,
    ) = backward_weights
    grad_out = cotangent[0]
    grad_inner = back_product(grad_out, down_full)
    sigmoid_gate = jax.nn.sigmoid(gate_act)
    grad_gate = (
        grad_inner * up_act * sigmoid_gate * (1.0 + gate_act * (1.0 - sigmoid_gate))
    ).astype(jnp.bfloat16)
    grad_up = (grad_inner * jax.nn.silu(gate_act)).astype(jnp.bfloat16)
    down_grad = outer_sum(inner_act, grad_out)
    gate_grad = outer_sum(normed_two, grad_gate)
    up_grad = outer_sum(normed_two, grad_up)
    grad_normed_two = back_product(grad_gate, gate_full) + back_product(grad_up, up_full)
    feed_gain_grad = jnp.sum(grad_normed_two * branch * scaling_two, 0)
    grad_branch = grad_out.astype(jnp.float32) + norm_back(
        branch, scaling_two, gain_two.astype(jnp.float32), grad_normed_two
    )
    grad_branch_low = grad_branch.astype(jnp.bfloat16)
    out_grad = outer_sum(attended, grad_branch_low)
    grad_attended = back_product(grad_branch_low, out_full).astype(jnp.bfloat16)
    head_count = queries.shape[1] // HEAD
    positions = keys_all.shape[0]
    grad_heads = grad_attended.reshape(frames, head_count, HEAD)
    query_heads = queries.reshape(frames, head_count, HEAD)
    key_heads = keys_all.reshape(positions, frames, head_count, HEAD)
    value_heads = values_all.reshape(positions, frames, head_count, HEAD)
    grad_soft = jnp.einsum(
        "fhe,jfhe->fhj", grad_heads, value_heads, preferred_element_type=jnp.float32
    )
    centre = jnp.sum(grad_soft * soft_weights, -1, keepdims=True)
    grad_scores = (soft_weights * (grad_soft - centre)).astype(jnp.bfloat16)
    grad_queries = jnp.einsum(
        "fhj,jfhe->fhe", grad_scores, key_heads, preferred_element_type=jnp.float32
    ) * HEAD ** (-0.5)
    grad_queries = grad_queries.astype(jnp.bfloat16).reshape(frames, -1)
    key_terms = jnp.einsum(
        "fhj,fhe->jfhe", grad_scores, query_heads, preferred_element_type=jnp.float32
    ) * HEAD ** (-0.5)
    value_terms = jnp.einsum(
        "fhj,fhe->jfhe", soft_low, grad_heads, preferred_element_type=jnp.float32
    )
    key_sum, value_sum = (
        lax.psum_scatter(
            key_terms.reshape(positions, frames, -1).astype(jnp.bfloat16),
            "pos",
            scatter_dimension=0,
            tiled=True,
        ).astype(jnp.float32),
        lax.psum_scatter(
            value_terms.reshape(positions, frames, -1).astype(jnp.bfloat16),
            "pos",
            scatter_dimension=0,
            tiled=True,
        ).astype(jnp.float32),
    )
    grad_keys = key_sum[0].astype(jnp.bfloat16)
    grad_values = value_sum[0].astype(jnp.bfloat16)
    query_grad = outer_sum(normed, grad_queries)
    key_grad = outer_sum(normed, grad_keys)
    value_grad = outer_sum(normed, grad_values)
    grad_normed = (
        back_product(grad_queries, query_full)
        + back_product(grad_keys, key_full)
        + back_product(grad_values, value_full)
    )
    attention_gain_grad = jnp.sum(grad_normed * hidden * scaling, 0)
    grad_hidden = grad_branch + norm_back(
        hidden, scaling, gain_one.astype(jnp.float32), grad_normed
    )
    grad_extended = jnp.pad(jnp.where(lag_rows == 0, grad_hidden, 0.0), ((2, 0), (0, 0)))
    grad_extended = grad_extended + jnp.pad(
        jnp.where(lag_rows == 1, grad_hidden, 0.0), ((1, 1), (0, 0))
    )
    grad_extended = grad_extended + jnp.pad(
        jnp.where(lag_rows == 2, grad_hidden, 0.0), ((0, 2), (0, 0))
    )
    rim_back = shifted(grad_extended[:2], "fr", -1)
    input_grad = (grad_extended[2:] + jnp.pad(rim_back, ((frames - 2, 0), (0, 0)))).astype(
        jnp.bfloat16
    )
    reduced = (
        lax.psum_scatter(
            query_grad[None].astype(jnp.bfloat16), "fr", scatter_dimension=1, tiled=True
        ).astype(jnp.float32),
        lax.psum_scatter(
            key_grad[None].astype(jnp.bfloat16), "fr", scatter_dimension=1, tiled=True
        ).astype(jnp.float32),
        lax.psum_scatter(
            value_grad[None].astype(jnp.bfloat16), "fr", scatter_dimension=1, tiled=True
        ).astype(jnp.float32),
        lax.psum_scatter(
            out_grad[None].astype(jnp.bfloat16), "fr", scatter_dimension=1, tiled=True
        ).astype(jnp.float32),
        lax.psum_scatter(
            gate_grad[None].astype(jnp.bfloat16), "fr", scatter_dimension=1, tiled=True
        ).astype(jnp.float32),
        lax.psum_scatter(
            up_grad[None].astype(jnp.bfloat16), "fr", scatter_dimension=1, tiled=True
        ).astype(jnp.float32),
        lax.psum_scatter(
            down_grad[None].astype(jnp.bfloat16), "fr", scatter_dimension=1, tiled=True
        ).astype(jnp.float32),
        lax.psum_scatter(
            attention_gain_grad[None].astype(jnp.bfloat16), "fr", scatter_dimension=1, tiled=True
        ).astype(jnp.float32),
        lax.psum_scatter(
            feed_gain_grad[None].astype(jnp.bfloat16), "fr", scatter_dimension=1, tiled=True
        ).astype(jnp.float32),
    )
    return (
        output[None],
        input_grad[None],
        reduced[0],
        reduced[1],
        reduced[2],
        reduced[3],
        reduced[4],
        reduced[5],
        reduced[6],
        reduced[7],
        reduced[8],
    )


def solution(mesh):
    return jax.shard_map(
        on_device,
        mesh=mesh,
        in_specs=(
            P("pos", "fr", None),
            P("fr", "pos"),
            P("pos", "fr", None),
            P("pos", "fr", None),
            P("pos", "fr", None),
            P("pos", "fr", None),
            P("pos", "fr", None),
            P("pos", "fr", None),
            P("pos", "fr", None),
            P("pos", "fr"),
            P("pos", "fr"),
            P("pos", "fr", None),
        ),
        out_specs=(
            P("pos", "fr", None),
            P("pos", "fr", None),
            P("pos", "fr", None),
            P("pos", "fr", None),
            P("pos", "fr", None),
            P("pos", "fr", None),
            P("pos", "fr", None),
            P("pos", "fr", None),
            P("pos", "fr", None),
            P("pos", "fr"),
            P("pos", "fr"),
        ),
        check_vma=False,
    )
```

profile of v0, /device:TPU:0, one launch (start us, length us, event | category | flops | bytes accessed | tf_op | source)
XLA Modules:
  0.0 1197.0 jit_solution(10028611180217504459)
XLA Ops:
  21.0 13.9 %all-gather.14.cloned.1.call-done = bf16[1,1024,1024]{2,1,0:T(8,128)(2,1)} async-done(((bf16[1,256,1024]{2,1,0:T(8,128)(2,1)}), bf16[1,1024,1024]{2,1,0:T(8,128)(2,1)}) %all-gather.14.cloned.1.call-update) | async-done | bytes 2097168 | tf_op jit(solution)/shard_map/all_gather | solution.py:113
  38.8 20.2 %all-gather.16.cloned.1.call-done = bf16[1,1024,1024]{2,1,0:T(8,128)(2,1)} async-done(((bf16[1,256,1024]{2,1,0:T(8,128)(2,1)}), bf16[1,1024,1024]{2,1,0:T(8,128)(2,1)}) %all-gather.16.cloned.1.call-update) | async-done | bytes 2097168 | tf_op jit(solution)/shard_map/all_gather | solution.py:114
  70.8 12.4 %all-gather.12.cloned.1.call-done = bf16[1,1024,1024]{2,1,0:T(8,128)(2,1)} async-done(((bf16[1,256,1024]{2,1,0:T(8,128)(2,1)}), bf16[1,1024,1024]{2,1,0:T(8,128)(2,1)}) %all-gather.12.cloned.1.call-update) | async-done | bytes 2097168 | tf_op jit(solution)/shard_map/all_gather | solution.py:112
  88.9 39.1 %all-gather.24.cloned.1.call-done = bf16[1,2816,1024]{2,1,0:T(8,128)(2,1)} async-done(((bf16[1,704,1024]{2,1,0:T(8,128)(2,1)}), bf16[1,2816,1024]{2,1,0:T(8,128)(2,1)}) %all-gather.24.cloned.1.call-update) | async-done | bytes 5767184 | tf_op jit(solution)/shard_map/all_gather | solution.py:118
  128.0 8.7 fusion
  136.7 118.4 %all-gather.26.cloned.1.call-done = bf16[4096,1024]{1,0:T(8,128)(2,1)} async-done(((bf16[512,1024]{1,0:T(8,128)(2,1)}), bf16[4096,1024]{1,0:T(8,128)(2,1)}) %all-gather.26.cloned.1.call-update) | async-done | bytes 8388624 | tf_op jit(solution)/shard_map/all_gather | solution.py:125
  255.1 11.3 copy.36
  266.4 12.2 %copy.73 = bf16[128,8,8,512]{3,2,1,0:T(8,128)(2,1)} copy(bf16[128,8,8,512]{3,1,2,0:T(8,128)(2,1)} %bitcast.166) | data formatting | bytes 16777216
  278.6 101.7 %all-gather.28.cloned.1.call-done = bf16[4096,1024]{1,0:T(8,128)(2,1)} async-done(((bf16[512,1024]{1,0:T(8,128)(2,1)}), bf16[4096,1024]{1,0:T(8,128)(2,1)}) %all-gather.28.cloned.1.call-update) | async-done | bytes 8388624 | tf_op jit(solution)/shard_map/all_gather | solution.py:126
  380.3 11.5 copy.37
  391.8 12.2 %copy.74 = bf16[128,8,8,512]{3,2,1,0:T(8,128)(2,1)} copy(bf16[128,8,8,512]{3,1,2,0:T(8,128)(2,1)} %bitcast.167) | data formatting | bytes 16777216
  410.7 11.3 multiply_reduce_fusion.2
  426.5 21.1 %all-gather.22.cloned.1.call-done = bf16[1,1024,2816]{2,1,0:T(8,128)(2,1)} async-done(((bf16[1,256,2816]{2,1,0:T(8,128)(2,1)}), bf16[1,1024,2816]{2,1,0:T(8,128)(2,1)}) %all-gather.22.cloned.1.call-update) | async-done | bytes 5767184 | tf_op jit(solution)/shard_map/all_gather | solution.py:117
  447.6 8.6 fusion.6
  456.3 36.3 %all-gather.20.cloned.1.call-done = bf16[1,1024,2816]{2,1,0:T(8,128)(2,1)} async-done(((bf16[1,256,2816]{2,1,0:T(8,128)(2,1)}), bf16[1,1024,2816]{2,1,0:T(8,128)(2,1)}) %all-gather.20.cloned.1.call-update) | async-done | bytes 5767184 | tf_op jit(solution)/shard_map/all_gather | solution.py:116
  492.6 12.0 multiply_convert_fusion.3
  539.7 8.4 multiply_convert_fusion
  555.4 10.1 multiply_reduce_fusion
  571.5 7.8 convert_bitcast_fusion
  579.4 7.8 convert_bitcast_fusion.2
  587.3 7.8 convert_bitcast_fusion.1
  595.4 91.0 %reduce-scatter.16.cloned.1.call-done = bf16[1,512,1024]{1,2,0:T(8,128)(2,1)} async-done(((bf16[8,512,1024]{1,2,0:T(8,128)(2,1)}), bf16[1,512,1024]{1,2,0:T(8,128)(2,1)}) %reduce-scatter.16.cloned.1.call-update) | async-done | bytes 1048592 | tf_op jit(solution)/shard_map/reduce_scatter | solution.py:207
  690.9 145.7 %reduce-scatter.18.cloned.1.call-done = bf16[1,512,1024]{1,2,0:T(8,128)(2,1)} async-done(((bf16[8,512,1024]{1,2,0:T(8,128)(2,1)}), bf16[1,512,1024]{1,2,0:T(8,128)(2,1)}) %reduce-scatter.18.cloned.1.call-update) | async-done | bytes 1048592 | tf_op jit(solution)/shard_map/reduce_scatter | solution.py:213
  852.7 7.7 fusion.60
  861.9 30.5 %reduce-scatter.26.cloned.1.call-done = bf16[1,256,1024]{2,1,0:T(8,128)(2,1)} async-done(((bf16[1,1024,1024]{2,1,0:T(8,128)(2,1)}), bf16[1,256,1024]{2,1,0:T(8,128)(2,1)}) %reduce-scatter.26.cloned.1.call-update) | async-done | bytes 524304 | tf_op jit(solution)/shard_map/reduce_scatter | solution.py:255
  894.5 31.4 %reduce-scatter.20.cloned.1.call-done = bf16[1,256,1024]{2,1,0:T(8,128)(2,1)} async-done(((bf16[1,1024,1024]{2,1,0:T(8,128)(2,1)}), bf16[1,256,1024]{2,1,0:T(8,128)(2,1)}) %reduce-scatter.20.cloned.1.call-update) | async-done | bytes 524304 | tf_op jit(solution)/shard_map/reduce_scatter | solution.py:246
  928.1 55.0 %reduce-scatter.32.cloned.1.call-done = bf16[1,704,1024]{2,1,0:T(8,128)(2,1)} async-done(((bf16[1,2816,1024]{2,1,0:T(8,128)(2,1)}), bf16[1,704,1024]{2,1,0:T(8,128)(2,1)}) %reduce-scatter.32.cloned.1.call-update) | async-done | bytes 1441808 | tf_op jit(solution)/shard_map/reduce_scatter | solution.py:264
  986.4 53.8 %reduce-scatter.28.cloned.1.call-done = bf16[1,256,2816]{2,1,0:T(8,128)(2,1)} async-done(((bf16[1,1024,2816]{2,1,0:T(8,128)(2,1)}), bf16[1,256,2816]{2,1,0:T(8,128)(2,1)}) %reduce-scatter.28.cloned.1.call-update) | async-done | bytes 1441808 | tf_op jit(solution)/shard_map/reduce_scatter | solution.py:258
  1043.4 54.0 %reduce-scatter.30.cloned.1.call-done = bf16[1,256,2816]{2,1,0:T(8,128)(2,1)} async-done(((bf16[1,1024,2816]{2,1,0:T(8,128)(2,1)}), bf16[1,256,2816]{2,1,0:T(8,128)(2,1)}) %reduce-scatter.30.cloned.1.call-update) | async-done | bytes 1441808 | tf_op jit(solution)/shard_map/reduce_scatter | solution.py:261
  1104.0 16.3 %reduce-scatter.34.cloned.1.call-done = bf16[256,1]{1,0:T(8,128)(2,1)} async-done(((bf16[1024,1]{1,0:T(8,128)(2,1)}), bf16[256,1]{1,0:T(8,128)(2,1)}) %reduce-scatter.34.cloned.1.call-update) | async-done | bytes 528
  1123.1 31.0 %reduce-scatter.22.cloned.1.call-done = bf16[1,256,1024]{2,1,0:T(8,128)(2,1)} async-done(((bf16[1,1024,1024]{2,1,0:T(8,128)(2,1)}), bf16[1,256,1024]{2,1,0:T(8,128)(2,1)}) %reduce-scatter.22.cloned.1.call-update) | async-done | bytes 524304 | tf_op jit(solution)/shard_map/reduce_scatter | solution.py:249
  1156.2 31.4 %reduce-scatter.24.cloned.1.call-done = bf16[1,256,1024]{2,1,0:T(8,128)(2,1)} async-done(((bf16[1,1024,1024]{2,1,0:T(8,128)(2,1)}), bf16[1,256,1024]{2,1,0:T(8,128)(2,1)}) %reduce-scatter.24.cloned.1.call-update) | async-done | bytes 524304 | tf_op jit(solution)/shard_map/reduce_scatter | solution.py:252
  (168 shorter events, 141.0 us)
Async XLA Ops:
  7.2 5.3 copy-start.22
  7.2 5.6 copy-start.20
  7.2 27.7 %all-gather.14.cloned.1.call-start = ((), (), s32[]{:S(2)}) async-start(), calls=%async_computation.12 | async-start | bytes 2621440 | tf_op jit(solution)/shard_map/all_gather | solution.py:113
  7.9 51.1 %all-gather.16.cloned.1.call-start = ((), (), s32[]{:S(2)}) async-start(), calls=%async_computation.13 | async-start | bytes 2621440 | tf_op jit(solution)/shard_map/all_gather | solution.py:114
  8.7 74.5 %all-gather.12.cloned.1.call-start = ((), (), s32[]{:S(2)}) async-start(), calls=%async_computation.11 | async-start | bytes 2621440 | tf_op jit(solution)/shard_map/all_gather | solution.py:112
  9.4 118.6 %all-gather.24.cloned.1.call-start = ((), (), s32[]{:S(2)}) async-start(), calls=%async_computation.17 | async-start | bytes 7208960 | tf_op jit(solution)/shard_map/all_gather | solution.py:118
  10.0 245.1 %all-gather.26.cloned.1.call-start = ((), (), s32[]{:S(2)}) async-start(), calls=%async_computation.27 | async-start | bytes 9437184 | tf_op jit(solution)/shard_map/all_gather | solution.py:125
  10.1 9.1 collective-permute-start
  12.7 26.1 %copy-start.16 = (pred[512]{0:T(512)(128)(4,1)}, pred[512]{0:T(512)(128)(4,1)S(1)}, u32[]{:S(2)}) copy-start(pred[512]{0:T(512)(128)(4,1)S(1)} %eq.52) | copy-start | bytes 1540
  12.8 25.9 %copy-start.18 = (pred[512]{0:T(512)(128)(4,1)}, pred[512]{0:T(512)(128)(4,1)S(1)}, u32[]{:S(2)}) copy-start(pred[512]{0:T(512)(128)(4,1)S(1)} %eq.55) | copy-start | bytes 1540
  38.8 341.5 %all-gather.28.cloned.1.call-start = ((), (), s32[]{:S(2)}) async-start(), calls=%async_computation.28 | async-start | bytes 9437184 | tf_op jit(solution)/shard_map/all_gather | solution.py:126
  62.9 359.1 %all-gather.18.cloned.1.call-start = ((), (), s32[]{:S(2)}) async-start(), calls=%async_computation.14 | async-start | bytes 2621440 | tf_op jit(solution)/shard_map/all_gather | solution.py:115
  63.7 384.0 %all-gather.22.cloned.1.call-start = ((), (), s32[]{:S(2)}) async-start(), calls=%async_computation.16 | async-start | bytes 7208960 | tf_op jit(solution)/shard_map/all_gather | solution.py:117
  64.4 428.2 %all-gather.20.cloned.1.call-start = ((), (), s32[]{:S(2)}) async-start(), calls=%async_computation.15 | async-start | bytes 7208960 | tf_op jit(solution)/shard_map/all_gather | solution.py:116
  65.2 621.2 %reduce-scatter.16.cloned.1.call-start = ((), (), s32[]{:S(2)}) async-start(), calls=%async_computation.18 | async-start | bytes 9437184 | tf_op jit(solution)/shard_map/reduce_scatter | solution.py:207
  88.9 315.1 %copy-start = (f32[512,16,64]{0,2,1:T(8,128)}, f32[512,16,64]{0,2,1:T(8,128)S(1)}, u32[]{:S(2)}) copy-start(f32[512,16,64]{0,2,1:T(8,128)S(1)} %bitcast_convert_fusion.1) | copy-start | bytes 6291460
  492.6 12.0 %copy-start.23 = (bf16[1,1024,2816]{2,1,0:T(8,128)(2,1)S(1)}, bf16[1,1024,2816]{2,1,0:T(8,128)(2,1)}, u32[]{:S(2)}) copy-start(bf16[1,1024,2816]{2,1,0:T(8,128)(2,1)} %all-gather.22.cloned.1.call-done) | copy-start | bytes 17301508
  531.3 7.4 copy-start.6
  538.7 297.9 %reduce-scatter.18.cloned.1.call-start = ((), (), s32[]{:S(2)}) async-start(), calls=%async_computation.19 | async-start | bytes 9437184 | tf_op jit(solution)/shard_map/reduce_scatter | solution.py:213
  548.0 312.3 %reduce-scatter.36.cloned.1.call-start = ((), (), s32[]{:S(2)}) async-start(), calls=%async_computation.30 | async-start | bytes 327680
  549.0 343.4 %reduce-scatter.26.cloned.1.call-start = ((), (), s32[]{:S(2)}) async-start(), calls=%async_computation.23 | async-start | bytes 2621440 | tf_op jit(solution)/shard_map/reduce_scatter | solution.py:255
  553.6 372.3 %reduce-scatter.20.cloned.1.call-start = ((), (), s32[]{:S(2)}) async-start(), calls=%async_computation.20 | async-start | bytes 2621440 | tf_op jit(solution)/shard_map/reduce_scatter | solution.py:246
  571.2 411.9 %reduce-scatter.32.cloned.1.call-start = ((), (), s32[]{:S(2)}) async-start(), calls=%async_computation.26 | async-start | bytes 7208960 | tf_op jit(solution)/shard_map/reduce_scatter | solution.py:264
  579.3 461.0 %reduce-scatter.28.cloned.1.call-start = ((), (), s32[]{:S(2)}) async-start(), calls=%async_computation.24 | async-start | bytes 7208960 | tf_op jit(solution)/shard_map/reduce_scatter | solution.py:258
  587.2 510.2 %reduce-scatter.30.cloned.1.call-start = ((), (), s32[]{:S(2)}) async-start(), calls=%async_computation.25 | async-start | bytes 7208960 | tf_op jit(solution)/shard_map/reduce_scatter | solution.py:261
  595.1 525.2 %reduce-scatter.34.cloned.1.call-start = ((), (), s32[]{:S(2)}) async-start(), calls=%async_computation.29 | async-start | bytes 327680
  844.2 309.8 %reduce-scatter.22.cloned.1.call-start = ((), (), s32[]{:S(2)}) async-start(), calls=%async_computation.21 | async-start | bytes 2621440 | tf_op jit(solution)/shard_map/reduce_scatter | solution.py:249
  848.4 339.2 %reduce-scatter.24.cloned.1.call-start = ((), (), s32[]{:S(2)}) async-start(), calls=%async_computation.22 | async-start | bytes 2621440 | tf_op jit(solution)/shard_map/reduce_scatter | solution.py:252
  1043.4 57.3 %copy-start.2 = (f32[512,1024]{1,0:T(8,128)S(1)}, f32[512,1024]{1,0:T(8,128)}, u32[]{:S(2)}) copy-start(f32[512,1024]{1,0:T(8,128)} %copy-done.1) | copy-start | bytes 6291460
  1043.4 57.3 %copy-start.15 = (f32[512]{0:T(512)S(1)}, f32[512]{0:T(512)}, u32[]{:S(2)}) copy-start(f32[512]{0:T(512)} %get-tuple-element.24) | copy-start | bytes 6148
  1043.4 57.3 %copy-start.17 = (pred[512]{0:T(512)(128)(4,1)S(1)}, pred[512]{0:T(512)(128)(4,1)}, u32[]{:S(2)}) copy-start(pred[512]{0:T(512)(128)(4,1)} %copy-done.16) | copy-start | bytes 1540
  1101.8 20.1 %collective-permute-start.1 = (f32[2,1024]{1,0:T(2,128)S(1)}, f32[2,1024]{1,0:T(2,128)S(1)}, u32[]{:S(2)}, u32[]{:S(2)}) collective-permute-start(f32[2,1024]{1,0:T(2,128)S(1)} %pad_add_fusion.1), channel_id=1, source_target_pairs={{1,0},{2,1},{3,2},{5,4},{6,5},{7,6},{9,8},{10,9},{11,10},{13,12},{... | collective-permute-start | bytes 24584 | tf_op jit(solution)/shard_map/ppermute | solution.py:14
  (17 other events, 40.8 us)
Sparse Core Ops, SparseCore 0:
  9.6 25.2 all-gather.13
  36.4 22.5 all-gather.15
  60.6 22.5 all-gather.11
  84.6 43.3 all-gather.23
  130.6 124.4 all-gather.25
  257.6 122.6 all-gather.27
  381.9 20.7 all-gather.17
  404.2 43.3 all-gather.21
  449.2 43.3 all-gather.19
  538.9 147.4 reduce-scatter.15
  690.0 146.5 reduce-scatter.17
  839.5 19.1 reduce-scatter.35
  861.2 31.1 reduce-scatter.25
  894.8 31.1 reduce-scatter.19
  928.4 54.7 reduce-scatter.31
  985.5 54.7 reduce-scatter.27
  1042.6 54.7 reduce-scatter.29
  1100.3 20.0 reduce-scatter.33
  1122.9 31.1 reduce-scatter.21
  1156.4 31.1 reduce-scatter.23
where the time goes:
time: 1200 us
  waiting for transfers between devices  908 us (76%)
  matrix products  110 us (9%)
  other arithmetic  84.5 us (7%)
  local copies, waits for them, and re-layouts  62.3 us (5%)
  between operations  15.2 us (1%)
    reduce_scatter x1, waiting for transfers between devices, on_device(): lax.psum_scatter(value_terms.reshape(positions, frames, -1).astype(jnp.bf...  146 us
    all_gather x1, waiting for transfers between devices, on_device(): lax.all_gather(key_rows[None], 'pos', axis=0, tiled=True)  118 us
    all_gather x1, waiting for transfers between devices, on_device(): lax.all_gather(value_rows[None], 'pos', axis=0, tiled=True)  102 us
    reduce_scatter x1, waiting for transfers between devices, on_device(): lax.psum_scatter(key_terms.reshape(positions, frames, -1).astype(jnp.bflo...  91 us
    reduce_scatter x1, waiting for transfers between devices, on_device(): lax.psum_scatter(down_grad[None].astype(jnp.bfloat16), 'fr', scatter_dime...  55 us
    reduce_scatter x1, waiting for transfers between devices, on_device(): lax.psum_scatter(up_grad[None].astype(jnp.bfloat16), 'fr', scatter_dimens...  54 us
    reduce_scatter x1, waiting for transfers between devices, on_device(): lax.psum_scatter(gate_grad[None].astype(jnp.bfloat16), 'fr', scatter_dime...  53.8 us
    dot_general x7, matrix products, product(): return jnp.dot(operand, weight, preferred_element_type=jnp.float32)  42.2 us
  transfers between devices with their start and end apart: 22, of which 18 were waited for; matrix products, arithmetic and copies ran while one was open for 17% of the time, Pallas kernels for 0%

commit v1 on v0

--- a/solution.py
+++ b/solution.py
@@ -6,6 +6,31 @@
 HEAD = 64
 EPSILON = 1e-06
 NEGATIVE = -1e30
+
+
+def try_all_the_table(mine_x, comm_axis):
+    next_value, z_new, formed = (
+        lax.axis_size(comm_axis),
+        lax.axis_index(comm_axis),
+        mine_x.shape[0],
+    )
+    samples = [(u, (u + 1) % next_value) for u in range(next_value)]
+    found = [(u, (u - 1) % next_value) for u in range(next_value)]
+    arr_now = jnp.zeros((*mine_x.shape[:0], next_value * formed, *mine_x.shape[1:]), mine_x.dtype)
+    arr_now = lax.dynamic_update_slice_in_dim(arr_now, mine_x, z_new * formed, axis=0)
+    main = low = mine_x
+    value_now = next_value // 2
+    for t in tuple(range(1, value_now + 1)):
+        main = lax.ppermute(main, comm_axis, samples)
+        arr_now = lax.dynamic_update_slice_in_dim(
+            arr_now, main, (z_new - t) % next_value * formed, axis=0
+        )
+        if t < next_value - value_now:
+            low = lax.ppermute(low, comm_axis, found)
+            arr_now = lax.dynamic_update_slice_in_dim(
+                arr_now, low, (z_new + t) % next_value * formed, axis=0
+            )
+    return arr_now
 
 
 def shifted(x, axis, by):
@@ -122,7 +147,7 @@
     forward_weights = tuple((shard_piece[0] for shard_piece in gathered))
     scaling, normed, queries, key_rows, value_rows = project_in(hidden, forward_weights)
     keys_all, values_all = (
-        lax.all_gather(key_rows[None], "pos", axis=0, tiled=True),
+        try_all_the_table(key_rows[None], comm_axis="pos"),
         lax.all_gather(value_rows[None], "pos", axis=0, tiled=True),
     )
     attended, logsum, soft_weights, soft_low = attend(queries, keys_all, values_all, position, None)

time: 1200 us -> 1250 us (1.042)
  local copies, waits for them, and re-layouts: 62.3 us -> 107 us
  waiting for transfers between devices: 908 us -> 876 us
  starting transfers between devices: 5.13 us -> 23.5 us
  matrix products: 110 us -> 126 us
    ppermute x0 -> x7, waiting for transfers between devices: none -> 155 us  [the longest x4 155 us: try_all_the_table(): main = lax.ppermute(main, comm_axis, samples)]
    all_gather x1, waiting for transfers between devices: 118 us -> 16.8 us  [on_device(): lax.all_gather(key_rows[None], 'pos', axis=0, tiled=True)]
    reduce_scatter x1, waiting for transfers between devices: 146 us -> 84.3 us  [on_device(): lax.psum_scatter(value_terms.reshape(positions, frames, -1).astype(jnp.bf...]
    reduce_scatter x1, waiting for transfers between devices: 91 us -> 146 us  [on_device(): lax.psum_scatter(key_terms.reshape(positions, frames, -1).astype(jnp.bflo...]
    all_gather x1, waiting for transfers between devices: 39.1 us -> 0.02 us  [on_device(): lax.all_gather(down_weight, 'fr', axis=1, tiled=True)]
    reduce_scatter x1, waiting for transfers between devices: 31.4 us -> 12.5 us  [on_device(): lax.psum_scatter(query_grad[None].astype(jnp.bfloat16), 'fr', scatter_dim...]
    ppermute x0 -> x7, starting transfers between devices: none -> 18.2 us  [the longest x4 9.24 us: try_all_the_table(): main = lax.ppermute(main, comm_axis, samples)]
    dot_general x7 -> x9, matrix products: 42.2 us -> 60.1 us  [product(): return jnp.dot(operand, weight, preferred_element_type=jnp.float32)]
  transfers between devices with their start and end apart: 22 -> 29, of which waited for: 18 -> 20; matrix products, arithmetic and copies ran while one was open for 17% -> 22% of each run, Pallas kernels for 0% -> 0%
where the time goes in v1:
time: 1250 us
  waiting for transfers between devices  876 us (70%)
  matrix products  126 us (10%)
  local copies, waits for them, and re-layouts  107 us (9%)
  other arithmetic  88.9 us (7%)
  starting transfers between devices  23.5 us (2%)
  between operations  15.1 us (1%)
    ppermute x4, waiting for transfers between devices, try_all_the_table(): main = lax.ppermute(main, comm_axis, samples)  155 us
    reduce_scatter x1, waiting for transfers between devices, on_device(): lax.psum_scatter(key_terms.reshape(positions, frames, -1).astype(jnp.bflo...  146 us
    all_gather x1, waiting for transfers between devices, on_device(): lax.all_gather(value_rows[None], 'pos', axis=0, tiled=True)  91.6 us
    reduce_scatter x1, waiting for transfers between devices, on_device(): lax.psum_scatter(value_terms.reshape(positions, frames, -1).astype(jnp.bf...  84.3 us
    dot_general x9, matrix products, product(): return jnp.dot(operand, weight, preferred_element_type=jnp.float32)  60.1 us
    reduce_scatter x1, waiting for transfers between devices, on_device(): lax.psum_scatter(gate_grad[None].astype(jnp.bfloat16), 'fr', scatter_dime...  55 us
    reduce_scatter x1, waiting for transfers between devices, on_device(): lax.psum_scatter(up_grad[None].astype(jnp.bfloat16), 'fr', scatter_dimens...  54 us
    reduce_scatter x1, waiting for transfers between devices, on_device(): lax.psum_scatter(down_grad[None].astype(jnp.bfloat16), 'fr', scatter_dime...  54 us
  transfers between devices with their start and end apart: 29, of which 20 were waited for; matrix products, arithmetic and copies ran while one was open for 22% of the time, Pallas kernels for 0%

profile of v1, /device:TPU:0, one launch (start us, length us, event | category | flops | bytes accessed | tf_op | source)
XLA Modules:
  0.0 1248.2 jit_solution(2889916876945914929)
XLA Ops:
  21.4 13.4 %all-gather.14.cloned.1.call-done = bf16[1,1024,1024]{2,1,0:T(8,128)(2,1)} async-done(((bf16[1,256,1024]{2,1,0:T(8,128)(2,1)}), bf16[1,1024,1024]{2,1,0:T(8,128)(2,1)}) %all-gather.14.cloned.1.call-update) | async-done | bytes 2097168 | tf_op jit(solution)/shard_map/all_gather | solution.py:138
  38.8 20.2 %all-gather.16.cloned.1.call-done = bf16[1,1024,1024]{2,1,0:T(8,128)(2,1)} async-done(((bf16[1,256,1024]{2,1,0:T(8,128)(2,1)}), bf16[1,1024,1024]{2,1,0:T(8,128)(2,1)}) %all-gather.16.cloned.1.call-update) | async-done | bytes 2097168 | tf_op jit(solution)/shard_map/all_gather | solution.py:139
  69.3 42.0 %collective-permute-done.1 = bf16[1,512,1024]{2,1,0:T(8,128)(2,1)} collective-permute-done((bf16[1,512,1024]{2,1,0:T(8,128)(2,1)S(1)}, bf16[1,512,1024]{2,1,0:T(8,128)(2,1)}, u32[]{:S(2)}, u32[]{:S(2)}) %collective-permute-start.1) | collective-permute-done | bytes 1048608 | tf_op jit(solution)/shard_map/ppermute | solution.py:24
  116.8 53.0 %collective-permute-done.3 = bf16[1,512,1024]{2,1,0:T(8,128)(2,1)S(1)} collective-permute-done((bf16[1,512,1024]{2,1,0:T(8,128)(2,1)}, bf16[1,512,1024]{2,1,0:T(8,128)(2,1)S(1)}, u32[]{:S(2)}, u32[]{:S(2)}) %collective-permute-start.3) | collective-permute-done | bytes 1048608 | tf_op jit(solution)/shard_map/ppermute | solution.py:24
  184.4 48.5 %collective-permute-done.5 = bf16[1,512,1024]{2,1,0:T(8,128)(2,1)} collective-permute-done((bf16[1,512,1024]{2,1,0:T(8,128)(2,1)S(1)}, bf16[1,512,1024]{2,1,0:T(8,128)(2,1)}, u32[]{:S(2)}, u32[]{:S(2)}) %collective-permute-start.5) | collective-permute-done | bytes 1048608 | tf_op jit(solution)/shard_map/ppermute | solution.py:24
  268.4 11.1 collective-permute-done.7
  291.3 8.9 fusion.2
  300.1 16.8 %all-gather.28.cloned.1.call-done = bf16[4096,1024]{1,0:T(8,128)(2,1)} async-done(((bf16[512,1024]{1,0:T(8,128)(2,1)}), bf16[4096,1024]{1,0:T(8,128)(2,1)}) %all-gather.28.cloned.1.call-update) | async-done | bytes 8388624 | tf_op jit(solution)/shard_map/all_gather | solution.py:172
  316.9 12.3 copy.61
  329.1 12.3 copy.111
  350.1 91.6 %all-gather.26.cloned.1.call-done = bf16[4096,1024]{1,0:T(8,128)(2,1)} async-done(((bf16[512,1024]{1,0:T(8,128)(2,1)}), bf16[4096,1024]{1,0:T(8,128)(2,1)}) %all-gather.26.cloned.1.call-update) | async-done | bytes 8388624 | tf_op jit(solution)/shard_map/all_gather | solution.py:151
  441.7 12.4 copy.60
  454.1 12.3 copy.110
  466.6 13.9 %fusion.1 = (bf16[512,16,64]{0,2,1:T(8,128)(2,1)}, bf16[512,16,64]{0,2,1:T(8,128)(2,1)}) fusion(f32[512,16,8]{0,2,1:T(8,128)S(1)} %copy-done.26, bf16[8,512,16,64]{1,0,3,2:T(8,128)(2,1)} %bitcast.187, f32[512,16,8]{0,2,1:T(8,128)S(1)} %copy.105), kind=kLoop, calls=%fused_computation.3 | loop fusion | flops 19922944 | bytes 11010048 | tf_op jit(solution)/shard_map/fhj,jfhe->fhe/dot_general | solution.py:93
  486.4 22.6 %all-gather.22.cloned.1.call-done = bf16[1,1024,2816]{2,1,0:T(8,128)(2,1)} async-done(((bf16[1,256,2816]{2,1,0:T(8,128)(2,1)}), bf16[1,1024,2816]{2,1,0:T(8,128)(2,1)}) %all-gather.22.cloned.1.call-update) | async-done | bytes 5767184 | tf_op jit(solution)/shard_map/all_gather | solution.py:142
  509.0 8.6 fusion.8
  517.6 36.3 %all-gather.20.cloned.1.call-done = bf16[1,1024,2816]{2,1,0:T(8,128)(2,1)} async-done(((bf16[1,256,2816]{2,1,0:T(8,128)(2,1)}), bf16[1,1024,2816]{2,1,0:T(8,128)(2,1)}) %all-gather.20.cloned.1.call-update) | async-done | bytes 5767184 | tf_op jit(solution)/shard_map/all_gather | solution.py:141
  554.0 11.7 multiply_convert_fusion.4
  606.6 8.7 multiply_reduce_fusion
  642.5 10.3 convert_bitcast_fusion
  652.8 84.3 %reduce-scatter.18.cloned.1.call-done = bf16[1,512,1024]{1,2,0:T(8,128)(2,1)} async-done(((bf16[8,512,1024]{1,2,0:T(8,128)(2,1)}), bf16[1,512,1024]{1,2,0:T(8,128)(2,1)}) %reduce-scatter.18.cloned.1.call-update) | async-done | bytes 1048592 | tf_op jit(solution)/shard_map/reduce_scatter | solution.py:238
  741.0 146.4 %reduce-scatter.16.cloned.1.call-done = bf16[1,512,1024]{1,2,0:T(8,128)(2,1)} async-done(((bf16[8,512,1024]{1,2,0:T(8,128)(2,1)}), bf16[1,512,1024]{1,2,0:T(8,128)(2,1)}) %reduce-scatter.16.cloned.1.call-update) | async-done | bytes 1048592 | tf_op jit(solution)/shard_map/reduce_scatter | solution.py:232
  907.7 7.8 fusion.16
  915.5 14.2 %fusion.76 = bf16[1,512,1024]{2,1,0:T(8,128)(2,1)} fusion(f32[512,1024]{1,0:T(8,128)S(1)} %copy-done.22, bf16[1,2816,1024]{2,1,0:T(8,128)(2,1)} %all-gather.24.cloned.1.call-done, f32[512,2816]{1,0:T(8,128)} %fusion.16, bf16[1,1024,2816]{2,1,0:T(8,128)(2,1)} %all-gather.22.cloned.1.call-done, f32[1024]{0:T(1024)S(1)} %bitcast.216, f32[512]{0:T(512)S(1)} %add_rsqrt_fusion.1), kind=kOutput, calls=%fused_computation.91 | convolution fusion | flops 5916852224 | bytes 20453376 | tf_op jit(solution)/shard_map/dot_general | solution.py:47
  931.2 12.5 %reduce-scatter.20.cloned.1.call-done = bf16[1,256,1024]{2,1,0:T(8,128)(2,1)} async-done(((bf16[1,1024,1024]{2,1,0:T(8,128)(2,1)}), bf16[1,256,1024]{2,1,0:T(8,128)(2,1)}) %reduce-scatter.20.cloned.1.call-update) | async-done | bytes 524304 | tf_op jit(solution)/shard_map/reduce_scatter | solution.py:271
  945.8 31.4 %reduce-scatter.26.cloned.1.call-done = bf16[1,256,1024]{2,1,0:T(8,128)(2,1)} async-done(((bf16[1,1024,1024]{2,1,0:T(8,128)(2,1)}), bf16[1,256,1024]{2,1,0:T(8,128)(2,1)}) %reduce-scatter.26.cloned.1.call-update) | async-done | bytes 524304 | tf_op jit(solution)/shard_map/reduce_scatter | solution.py:280
  979.4 55.0 %reduce-scatter.28.cloned.1.call-done = bf16[1,256,2816]{2,1,0:T(8,128)(2,1)} async-done(((bf16[1,1024,2816]{2,1,0:T(8,128)(2,1)}), bf16[1,256,2816]{2,1,0:T(8,128)(2,1)}) %reduce-scatter.28.cloned.1.call-update) | async-done | bytes 1441808 | tf_op jit(solution)/shard_map/reduce_scatter | solution.py:283
  1037.5 54.0 %reduce-scatter.30.cloned.1.call-done = bf16[1,256,2816]{2,1,0:T(8,128)(2,1)} async-done(((bf16[1,1024,2816]{2,1,0:T(8,128)(2,1)}), bf16[1,256,2816]{2,1,0:T(8,128)(2,1)}) %reduce-scatter.30.cloned.1.call-update) | async-done | bytes 1441808 | tf_op jit(solution)/shard_map/reduce_scatter | solution.py:286
  1094.7 54.0 %reduce-scatter.32.cloned.1.call-done = bf16[1,704,1024]{2,1,0:T(8,128)(2,1)} async-done(((bf16[1,2816,1024]{2,1,0:T(8,128)(2,1)}), bf16[1,704,1024]{2,1,0:T(8,128)(2,1)}) %reduce-scatter.32.cloned.1.call-update) | async-done | bytes 1441808 | tf_op jit(solution)/shard_map/reduce_scatter | solution.py:289
  1155.5 16.2 %reduce-scatter.34.cloned.1.call-done = bf16[256,1]{1,0:T(8,128)(2,1)} async-done(((bf16[1024,1]{1,0:T(8,128)(2,1)}), bf16[256,1]{1,0:T(8,128)(2,1)}) %reduce-scatter.34.cloned.1.call-update) | async-done | bytes 528
  1174.4 31.0 %reduce-scatter.22.cloned.1.call-done = bf16[1,256,1024]{2,1,0:T(8,128)(2,1)} async-done(((bf16[1,1024,1024]{2,1,0:T(8,128)(2,1)}), bf16[1,256,1024]{2,1,0:T(8,128)(2,1)}) %reduce-scatter.22.cloned.1.call-update) | async-done | bytes 524304 | tf_op jit(solution)/shard_map/reduce_scatter | solution.py:274
  1207.5 31.5 %reduce-scatter.24.cloned.1.call-done = bf16[1,256,1024]{2,1,0:T(8,128)(2,1)} async-done(((bf16[1,1024,1024]{2,1,0:T(8,128)(2,1)}), bf16[1,256,1024]{2,1,0:T(8,128)(2,1)}) %reduce-scatter.24.cloned.1.call-update) | async-done | bytes 524304 | tf_op jit(solution)/shard_map/reduce_scatter | solution.py:277
  (242 shorter events, 228.0 us)
Async XLA Ops:
  7.2 27.7 %all-gather.14.cloned.1.call-start = ((), (), s32[]{:S(2)}) async-start(), calls=%async_computation.12 | async-start | bytes 2621440 | tf_op jit(solution)/shard_map/all_gather | solution.py:138
  7.9 51.1 %all-gather.16.cloned.1.call-start = ((), (), s32[]{:S(2)}) async-start(), calls=%async_computation.13 | async-start | bytes 2621440 | tf_op jit(solution)/shard_map/all_gather | solution.py:139
  8.7 171.5 %all-gather.12.cloned.1.call-start = ((), (), s32[]{:S(2)}) async-start(), calls=%async_computation.11 | async-start | bytes 2621440 | tf_op jit(solution)/shard_map/all_gather | solution.py:137
  9.4 281.8 %all-gather.24.cloned.1.call-start = ((), (), s32[]{:S(2)}) async-start(), calls=%async_computation.17 | async-start | bytes 7208960 | tf_op jit(solution)/shard_map/all_gather | solution.py:143
  10.0 306.9 %all-gather.28.cloned.1.call-start = ((), (), s32[]{:S(2)}) async-start(), calls=%async_computation.28 | async-start | bytes 9437184 | tf_op jit(solution)/shard_map/all_gather | solution.py:172
  10.1 9.6 collective-permute-start
  38.8 402.9 %all-gather.26.cloned.1.call-start = ((), (), s32[]{:S(2)}) async-start(), calls=%async_computation.27 | async-start | bytes 9437184 | tf_op jit(solution)/shard_map/all_gather | solution.py:151
  62.9 109.3 %copy-start.36 = (bf16[1,256]{1,0:T(2,128)(2,1)S(1)}, bf16[1,256]{1,0:T(2,128)(2,1)}, u32[]{:S(2)}) copy-start(bf16[1,256]{1,0:T(2,128)(2,1)} %param.22) | copy-start | bytes 1540
  62.9 417.6 %all-gather.18.cloned.1.call-start = ((), (), s32[]{:S(2)}) async-start(), calls=%async_computation.14 | async-start | bytes 2621440 | tf_op jit(solution)/shard_map/all_gather | solution.py:140
  63.7 445.3 %all-gather.22.cloned.1.call-start = ((), (), s32[]{:S(2)}) async-start(), calls=%async_computation.16 | async-start | bytes 7208960 | tf_op jit(solution)/shard_map/all_gather | solution.py:142
  64.4 489.5 %all-gather.20.cloned.1.call-start = ((), (), s32[]{:S(2)}) async-start(), calls=%async_computation.15 | async-start | bytes 7208960 | tf_op jit(solution)/shard_map/all_gather | solution.py:141
  64.5 46.8 %collective-permute-start.1 = (bf16[1,512,1024]{2,1,0:T(8,128)(2,1)S(1)}, bf16[1,512,1024]{2,1,0:T(8,128)(2,1)}, u32[]{:S(2)}, u32[]{:S(2)}) collective-permute-start(bf16[1,512,1024]{2,1,0:T(8,128)(2,1)S(1)} %bitcast.196), channel_id=1, source_target_pairs={{0,4},{4,8},{8,12},{12,16},{16,20},{20,24},{24,28},{28,0},{1,5},{5... | collective-permute-start | bytes 3145736 | tf_op jit(solution)/shard_map/ppermute | solution.py:24
  66.0 47.9 %collective-permute-start.2 = (bf16[1,512,1024]{2,1,0:T(8,128)(2,1)S(1)}, bf16[1,512,1024]{2,1,0:T(8,128)(2,1)}, u32[]{:S(2)}, u32[]{:S(2)}) collective-permute-start(bf16[1,512,1024]{2,1,0:T(8,128)(2,1)S(1)} %bitcast.197), channel_id=1, source_target_pairs={{0,28},{4,0},{8,4},{12,8},{16,12},{20,16},{24,20},{28,24},{1,29},{... | collective-permute-start | bytes 3145736 | tf_op jit(solution)/shard_map/ppermute | solution.py:29
  111.3 58.5 %collective-permute-start.3 = (bf16[1,512,1024]{2,1,0:T(8,128)(2,1)}, bf16[1,512,1024]{2,1,0:T(8,128)(2,1)S(1)}, u32[]{:S(2)}, u32[]{:S(2)}) collective-permute-start(bf16[1,512,1024]{2,1,0:T(8,128)(2,1)} %collective-permute-done.1), channel_id=1, source_target_pairs={{0,4},{4,8},{8,12},{12,16},{16,20},{20,24},{24,28},{28,0},{1,5},{5... | collective-permute-start | bytes 3145736 | tf_op jit(solution)/shard_map/ppermute | solution.py:24
  113.9 623.2 %reduce-scatter.18.cloned.1.call-start = ((), (), s32[]{:S(2)}) async-start(), calls=%async_computation.19 | async-start | bytes 9437184 | tf_op jit(solution)/shard_map/reduce_scatter | solution.py:238
  114.0 63.3 %collective-permute-start.4 = (bf16[1,512,1024]{2,1,0:T(8,128)(2,1)}, bf16[1,512,1024]{2,1,0:T(8,128)(2,1)}, u32[]{:S(2)}, u32[]{:S(2)}) collective-permute-start(bf16[1,512,1024]{2,1,0:T(8,128)(2,1)} %collective-permute-done.2), channel_id=1, source_target_pairs={{0,28},{4,0},{8,4},{12,8},{16,12},{20,16},{24,20},{28,24},{1,29},{... | collective-permute-start | bytes 3145736 | tf_op jit(solution)/shard_map/ppermute | solution.py:29
  169.8 63.1 %collective-permute-start.5 = (bf16[1,512,1024]{2,1,0:T(8,128)(2,1)S(1)}, bf16[1,512,1024]{2,1,0:T(8,128)(2,1)}, u32[]{:S(2)}, u32[]{:S(2)}) collective-permute-start(bf16[1,512,1024]{2,1,0:T(8,128)(2,1)S(1)} %collective-permute-done.3), channel_id=1, source_target_pairs={{0,4},{4,8},{8,12},{12,16},{16,20},{20,24},{24,28},{28,0},{1,5},{5... | collective-permute-start | bytes 3145736 | tf_op jit(solution)/shard_map/ppermute | solution.py:24
  177.3 85.5 %collective-permute-start.6 = (bf16[1,512,1024]{2,1,0:T(8,128)(2,1)}, bf16[1,512,1024]{2,1,0:T(8,128)(2,1)}, u32[]{:S(2)}, u32[]{:S(2)}) collective-permute-start(bf16[1,512,1024]{2,1,0:T(8,128)(2,1)} %collective-permute-done.4), channel_id=1, source_target_pairs={{0,28},{4,0},{8,4},{12,8},{16,12},{20,16},{24,20},{28,24},{1,29},{... | collective-permute-start | bytes 3145736 | tf_op jit(solution)/shard_map/ppermute | solution.py:29
  232.9 46.6 %collective-permute-start.7 = (bf16[1,512,1024]{2,1,0:T(8,128)(2,1)}, bf16[1,512,1024]{2,1,0:T(8,128)(2,1)}, u32[]{:S(2)}, u32[]{:S(2)}) collective-permute-start(bf16[1,512,1024]{2,1,0:T(8,128)(2,1)} %collective-permute-done.5), channel_id=1, source_target_pairs={{0,4},{4,8},{8,12},{12,16},{16,20},{20,24},{24,28},{28,0},{1,5},{5... | collective-permute-start | bytes 3145736 | tf_op jit(solution)/shard_map/ppermute | solution.py:24
  589.5 297.9 %reduce-scatter.16.cloned.1.call-start = ((), (), s32[]{:S(2)}) async-start(), calls=%async_computation.18 | async-start | bytes 9437184 | tf_op jit(solution)/shard_map/reduce_scatter | solution.py:232
  604.6 325.1 %reduce-scatter.36.cloned.1.call-start = ((), (), s32[]{:S(2)}) async-start(), calls=%async_computation.30 | async-start | bytes 327680
  616.5 327.1 %reduce-scatter.20.cloned.1.call-start = ((), (), s32[]{:S(2)}) async-start(), calls=%async_computation.20 | async-start | bytes 2621440 | tf_op jit(solution)/shard_map/reduce_scatter | solution.py:271
  620.6 356.6 %reduce-scatter.26.cloned.1.call-start = ((), (), s32[]{:S(2)}) async-start(), calls=%async_computation.23 | async-start | bytes 2621440 | tf_op jit(solution)/shard_map/reduce_scatter | solution.py:280
  626.1 408.3 %reduce-scatter.28.cloned.1.call-start = ((), (), s32[]{:S(2)}) async-start(), calls=%async_computation.24 | async-start | bytes 7208960 | tf_op jit(solution)/shard_map/reduce_scatter | solution.py:283
  634.2 457.4 %reduce-scatter.30.cloned.1.call-start = ((), (), s32[]{:S(2)}) async-start(), calls=%async_computation.25 | async-start | bytes 7208960 | tf_op jit(solution)/shard_map/reduce_scatter | solution.py:286
  641.3 507.4 %reduce-scatter.32.cloned.1.call-start = ((), (), s32[]{:S(2)}) async-start(), calls=%async_computation.26 | async-start | bytes 7208960 | tf_op jit(solution)/shard_map/reduce_scatter | solution.py:289
  652.7 84.4 %copy-start.41 = (bf16[1,1024,1024]{2,1,0:T(8,128)(2,1)S(1)}, bf16[1,1024,1024]{2,1,0:T(8,128)(2,1)}, u32[]{:S(2)}) copy-start(bf16[1,1024,1024]{2,1,0:T(8,128)(2,1)} %all-gather.16.cloned.1.call-done) | copy-start | bytes 6291460
  652.8 518.9 %reduce-scatter.34.cloned.1.call-start = ((), (), s32[]{:S(2)}) async-start(), calls=%async_computation.29 | async-start | bytes 327680
  740.9 149.8 %copy-start.9 = (bf16[512,16,64]{0,2,1:T(8,128)(2,1)S(1)}, bf16[512,16,64]{0,2,1:T(8,128)(2,1)}, u32[]{:S(2)}) copy-start(bf16[512,16,64]{0,2,1:T(8,128)(2,1)} %multiply_convert_fusion.7) | copy-start | bytes 3145732
  894.9 310.5 %reduce-scatter.22.cloned.1.call-start = ((), (), s32[]{:S(2)}) async-start(), calls=%async_computation.21 | async-start | bytes 2621440 | tf_op jit(solution)/shard_map/reduce_scatter | solution.py:274
  897.8 341.2 %reduce-scatter.24.cloned.1.call-start = ((), (), s32[]{:S(2)}) async-start(), calls=%async_computation.22 | async-start | bytes 2621440 | tf_op jit(solution)/shard_map/reduce_scatter | solution.py:277
  1153.2 19.9 %collective-permute-start.8 = (f32[2,1024]{1,0:T(2,128)S(1)}, f32[2,1024]{1,0:T(2,128)S(1)}, u32[]{:S(2)}, u32[]{:S(2)}) collective-permute-start(f32[2,1024]{1,0:T(2,128)S(1)} %pad_add_fusion.1), channel_id=1, source_target_pairs={{1,0},{2,1},{3,2},{5,4},{6,5},{7,6},{9,8},{10,9},{11,10},{13,12},{... | collective-permute-start | bytes 24584 | tf_op jit(solution)/shard_map/ppermute | solution.py:39
  (43 other events, 366.9 us)
Sparse Core Ops, SparseCore 0:
  9.6 25.2 all-gather.13
  36.4 22.5 all-gather.15
  60.6 22.5 all-gather.11
  84.6 43.3 all-gather.23
  130.6 186.2 all-gather.27
  319.4 122.2 all-gather.25
  443.2 20.7 all-gather.17
  465.6 43.3 all-gather.21
  510.6 43.3 all-gather.19
  589.6 147.4 reduce-scatter.17
  740.7 146.5 reduce-scatter.15
  890.2 19.1 reduce-scatter.35
  912.5 31.1 reduce-scatter.19
  946.1 31.1 reduce-scatter.25
  979.6 54.7 reduce-scatter.27
  1036.8 54.7 reduce-scatter.29
  1093.9 54.7 reduce-scatter.31
  1151.6 20.0 reduce-scatter.33
  1174.2 31.1 reduce-scatter.21
  1207.8 31.1 reduce-scatter.23
